TPU v7x, 256 devices: a whole 4x4x8 slice. The times are simulated.
256 devices in a mesh: rep: 16 (over z, y_hi), exp: 16 (over y_lo, x, core).
Axes of the slice: x: 4, y: 4 (y_hi: 2, y_lo: 2; y = y_hi * 2 + y_lo), z: 8, core: 2. Of those that a mesh axis runs over, the one named last changes fastest.
Arguments:
- tokens: bfloat16 [8192, 2048], P(('rep', 'exp')), may hold values from -6 to 6
- attend_weight: bfloat16 [2048, 16, 256], P(None, 'exp'), may hold values from -0.125 to 0.125
- value_weight: bfloat16 [2048, 32, 256], P(None, 'exp'), may hold values from -0.125 to 0.125
- rate_weight: bfloat16 [2048, 32, 2], P(None, 'exp'), may hold values from -0.125 to 0.125
- decay_rate: float32 [32], P('exp'), may hold values from 0.002 to 0.2
- output_weight: bfloat16 [32, 128, 2048], P('exp'), may hold values from -0.09375 to 0.09375
- state_cache: float32 [128, 32, 128, 128], P('rep', 'exp'), may hold values from -2.4 to 2.4
- resume_from: int32 [128], replicated, may hold values from 0 to 127, as said below
- expert_index: int32 [8192, 10], P(('rep', 'exp')), may hold values from 0 to 15, all different within a row; in each aligned block of 32 rows (0 to 31, 32 to 63, ...) at most 32 rows name the same one
- route_weight: float32 [8192, 10], P(('rep', 'exp')), may hold values from 0.02 to 0.3
- expert_inner: bfloat16 [16, 2048, 1024], P('exp'), may hold values from -0.125 to 0.125
- expert_outer: bfloat16 [16, 512, 2048], P('exp'), may hold values from -0.25 to 0.25
Outputs:
- layer_output: bfloat16 [8192, 2048], P(('rep', 'exp'))
- final_state: float32 [128, 32, 128, 128], P('rep', 'exp')
Inputs may be any that keep to these rules, and one draw needn't show every extreme that they name: `resume_from`: entry r * 8 + b is the cache row of trajectory b of group r; cache row c belongs to group c // 8. The 8 trajectories of one group take their rows from 8 different groups; a row may serve several groups. `expert_index`: each row names 10 different experts.
All inputs are finite; a program needn't handle non-finite values.
Results may differ from a plain program's by a relative error of at most 0.013.
Values may be sent and summed in bfloat16 or wider, within the bound.
No kernel may reach another device: no remote copies, remote signals or barrier semaphores. Data moves between devices by JAX's collectives and lax.ppermute only.
A program may use at most 128 MiB of HBM per device.

v0:
```python
from functools import partial
import jax
import jax.numpy as jnp
from jax import lax
from jax.sharding import PartitionSpec as P

EPSILON = 1e-06
HIGHEST = lax.Precision.HIGHEST


def rms_scale(values):
    return values * lax.rsqrt(jnp.mean(values * values, axis=-1, keepdims=True) + EPSILON)


def unit_length(values):
    return values * lax.rsqrt(jnp.sum(values * values, axis=-1, keepdims=True) + EPSILON)


def head_inputs(attend_part, value_part, rate_part, key_heads, value_heads, decay_rate):
    count = attend_part.shape[0]
    key_size = attend_part.shape[1] // (2 * key_heads)
    value_size = value_part.shape[1] // (2 * value_heads)
    paired = attend_part.reshape(count, key_heads, 2, key_size)
    repeat = value_heads // key_heads
    query = jnp.repeat(unit_length(paired[:, :, 0]), repeat, axis=1) * key_size ** (-0.5)
    key_rows = jnp.repeat(unit_length(paired[:, :, 1]), repeat, axis=1)
    value_pair = value_part.reshape(count, value_heads, 2, value_size)
    rate_pair = rate_part.reshape(count, value_heads, 2)
    beta_rows = jax.nn.sigmoid(rate_pair[:, :, 1])
    log_decay = -decay_rate[None, :] * jax.nn.softplus(rate_pair[:, :, 0])
    return (query, key_rows, value_pair[:, :, 0], value_pair[:, :, 1], beta_rows, log_decay)


def block_step(state, packed):
    query, key_rows, value_rows, beta_rows, log_decay = packed
    summed = jnp.cumsum(log_decay, axis=-1)
    width = summed.shape[-1]
    row_iota = lax.broadcasted_iota(jnp.int32, (width, width), 0)
    col_iota = lax.broadcasted_iota(jnp.int32, (width, width), 1)
    spread = summed[..., :, None] - summed[..., None, :]
    ratio = jnp.where(col_iota <= row_iota, jnp.exp(jnp.minimum(spread, 0.0)), 0.0)
    key_products = jnp.einsum("bhik,bhjk->bhij", key_rows, key_rows, precision=HIGHEST)
    below = jnp.where(col_iota < row_iota, beta_rows[..., :, None] * ratio * key_products, 0.0)
    system = below + jnp.eye(width, dtype=jnp.float32)
    carried = jnp.einsum("bhik,bhvk->bhiv", key_rows, state, precision=HIGHEST)
    right_side = beta_rows[..., None] * (value_rows - jnp.exp(summed)[..., None] * carried)
    solver = jax.vmap(partial(jax.scipy.linalg.solve_triangular, lower=True, unit_diagonal=True))
    updates = solver(
        system.reshape(-1, width, width), right_side.reshape(-1, width, right_side.shape[-1])
    ).reshape(right_side.shape)
    query_keys = jnp.einsum("bhik,bhjk->bhij", query, key_rows, precision=HIGHEST)
    readout = jnp.exp(summed)[..., None] * jnp.einsum(
        "bhik,bhvk->bhiv", query, state, precision=HIGHEST
    )
    readout = readout + jnp.einsum(
        "bhij,bhjv->bhiv", ratio * query_keys, updates, precision=HIGHEST
    )
    closing = summed[..., -1:]
    tail = jnp.exp(closing - summed)
    new_state = jnp.exp(closing)[..., None] * state + jnp.einsum(
        "bhjv,bhjk->bhvk", updates * tail[..., None], key_rows, precision=HIGHEST
    )
    return (new_state, readout)


def local(
    tokens,
    attend_weight,
    value_weight,
    rate_weight,
    decay_rate,
    output_weight,
    state_cache,
    resume_from,
    expert_index,
    route_weight,
    expert_inner,
    expert_outer,
):
    model = tokens.shape[1]
    key_heads = attend_weight.shape[1]
    value_heads = value_weight.shape[1]
    attend_flat = attend_weight.reshape(model, -1)
    value_flat = value_weight.reshape(model, -1)
    rate_flat = rate_weight.reshape(model, -1)
    residual = tokens.astype(jnp.float32)
    normed = rms_scale(residual).astype(jnp.bfloat16)
    piece = lax.all_gather(normed, "exp", axis=0, tiled=True)
    projected = jnp.concatenate(
        [
            jnp.dot(piece, attend_flat, preferred_element_type=jnp.float32),
            jnp.dot(piece, value_flat, preferred_element_type=jnp.float32),
            jnp.dot(piece, rate_flat, preferred_element_type=jnp.float32),
        ],
        axis=1,
    )
    first_cut = attend_flat.shape[1]
    second_cut = first_cut + value_flat.shape[1]
    query, key_rows, value_rows, gate_rows, beta_rows, log_decay = head_inputs(
        projected[:, :first_cut],
        projected[:, first_cut:second_cut],
        projected[:, second_cut:],
        key_heads,
        value_heads,
        decay_rate,
    )
    trajs = state_cache.shape[0]
    myself = lax.axis_index("rep")
    my_rows = lax.dynamic_slice_in_dim(resume_from, myself * trajs, trajs)
    every_cache = lax.all_gather(
        state_cache.astype(jnp.bfloat16), "rep", axis=0, tiled=True
    ).astype(state_cache.dtype)
    start = jnp.take(every_cache, my_rows, axis=0)
    length = projected.shape[0] // trajs
    block = min(64, length)
    blocks = length // block

    def arrange(values):
        shaped = values.reshape((trajs, blocks, block) + values.shape[1:])
        return jnp.moveaxis(jnp.moveaxis(shaped, 3, 1), 2, 0)

    final_state, readout = lax.scan(
        block_step,
        start,
        (
            arrange(query),
            arrange(key_rows),
            arrange(value_rows),
            arrange(beta_rows),
            arrange(log_decay),
        ),
    )
    readout = jnp.transpose(readout, (1, 0, 3, 2, 4)).reshape(value_rows.shape)
    gated = (
        (rms_scale(readout) * jax.nn.silu(gate_rows))
        .astype(jnp.bfloat16)
        .reshape(readout.shape[0], -1)
    )
    output_flat = output_weight.reshape(-1, model)
    row_count = tokens.shape[0]
    attended = lax.psum_scatter(
        jnp.dot(gated, output_flat, preferred_element_type=jnp.float32).astype(jnp.bfloat16),
        "exp",
        scatter_dimension=0,
        tiled=True,
    ).astype(jnp.float32)
    hidden = residual + attended
    hidden_normed = rms_scale(hidden).astype(jnp.bfloat16)
    top_count = expert_index.shape[1]
    local_experts = expert_inner.shape[0]
    total_experts = lax.axis_size("exp") * local_experts
    flat_index = expert_index.reshape(-1)
    one_hot = (flat_index[:, None] == jnp.arange(total_experts, dtype=jnp.int32)[None, :]).astype(
        jnp.int32
    )
    earlier = jnp.cumsum(one_hot, axis=0) - one_hot
    slot_of_pair = jnp.sum(earlier * one_hot, axis=1)
    position = flat_index * row_count + slot_of_pair
    owner = jnp.arange(row_count * top_count, dtype=jnp.int32) // top_count
    table = jnp.full((total_experts * row_count,), row_count, jnp.int32).at[position].set(owner)
    padded = jnp.concatenate([hidden_normed, jnp.zeros((1, model), jnp.bfloat16)], axis=0)
    outgoing_rows = jnp.take(padded, table, axis=0).reshape(
        lax.axis_size("exp"), local_experts, row_count, model
    )
    inner = expert_outer.shape[1]
    both_parts = jnp.einsum(
        "semd,edf->semf",
        lax.all_to_all(outgoing_rows, "exp", split_axis=0, concat_axis=0, tiled=True),
        expert_inner,
        preferred_element_type=jnp.float32,
    )
    activated = (jax.nn.silu(both_parts[..., :inner]) * both_parts[..., inner:]).astype(
        jnp.bfloat16
    )
    produced = jnp.einsum(
        "semf,efd->semd", activated, expert_outer, preferred_element_type=jnp.float32
    ).astype(jnp.bfloat16)
    returned = lax.all_to_all(produced, "exp", split_axis=0, concat_axis=0, tiled=True)
    pair_output = jnp.take(
        returned.reshape(total_experts * row_count, model), position, axis=0
    ).reshape(row_count, top_count, model)
    expert_sum = jnp.einsum(
        "rt,rtd->rd", route_weight, pair_output.astype(jnp.float32), precision=HIGHEST
    )
    layer_output = (hidden + expert_sum).astype(jnp.bfloat16)
    return (layer_output, final_state)


def solution(mesh):
    in_specs = (
        P(("rep", "exp"), None),
        P(None, "exp", None),
        P(None, "exp", None),
        P(None, "exp", None),
        P("exp"),
        P("exp", None, None),
        P("rep", "exp", None, None),
        P(),
        P(("rep", "exp"), None),
        P(("rep", "exp"), None),
        P("exp", None, None),
        P("exp", None, None),
    )
    out_specs = (P(("rep", "exp"), None), P("rep", "exp", None, None))
    return jax.shard_map(local, mesh=mesh, in_specs=in_specs, out_specs=out_specs, check_vma=False)
```

profile of v0, /device:TPU:2, one launch (start us, length us, event | category | flops | bytes accessed | tf_op | source)
XLA Modules:
  0.0 379.0 jit_solution(10832503527195283775)
XLA Ops:
  7.2 1.2 fusion.41
  8.4 1.7 fusion.42
  10.1 2.1 convert_element_type.57
  12.3 3.4 copy.105
  15.7 4.1 %copy.84 = bf16[512,2048]{1,0:T(8,128)(2,1)} copy(bf16[512,2048]{0,1:T(8,128)(2,1)} %bitcast.128) | data formatting | bytes 4194304 | tf_op jit(solution)/shard_map/dot_general | solution.py:92
  19.8 1.4 copy.101
  21.5 27.9 %all-gather.3.cloned.1.call-done = bf16[512,2048]{1,0:T(8,128)(2,1)} async-done(((bf16[32,2048]{1,0:T(8,128)(2,1)}), bf16[512,2048]{1,0:T(8,128)(2,1)}) %all-gather.3.cloned.1.call-update) | async-done | bytes 2097168 | tf_op jit(solution)/shard_map/all_gather | solution.py:88
  49.4 2.6 fusion.22
  52.3 2.2 fusion.9
  55.3 3.5 fusion.3
  58.8 1.0 copy-done.11
  59.8 0.9 slice.67
  62.2 1.0 fusion.26
  63.2 0.8 select_add_fusion
  64.0 80.0 %custom-call.5 = f32[16,1,64,64]{2,3,1,0:T(8,128)} custom-call(f32[16,1,64,64]{3,2,1,0:T(8,128)} %select_add_fusion), custom_call_target="InvertDiagBlocksLowerTriangular" | custom-call | tf_op jit(solution)/shard_map/while/body/eval_jaxpr/vmap(jit(_solve_triangular))/triangular_solve | solution.py:48
  144.2 1.7 convolution_multiply_fusion.3
  145.9 42.7 %all-gather.5.cloned.1.call-done = bf16[128,2,128,128]{3,2,1,0:T(8,128)(2,1)} async-done(((bf16[8,2,128,128]{3,2,1,0:T(8,128)(2,1)}), bf16[128,2,128,128]{3,2,1,0:T(8,128)(2,1)}) %all-gather.5.cloned.1.call-update) | async-done | bytes 8388624 | tf_op jit(solution)/shard_map/all_gather | solution.py:110
  188.7 11.2 %convert_element_type.58 = f32[128,2,128,128]{3,2,1,0:T(8,128)} convert(bf16[128,2,128,128]{3,2,1,0:T(8,128)(2,1)} %all-gather.5.cloned.1.call-done) | non-fusion elementwise | flops 4194304 | bytes 25165824 | tf_op jit(solution)/shard_map/convert_element_type | solution.py:112
  199.9 6.4 %gather_fusion = f32[8,2,128,128]{3,2,1,0:T(8,128)S(1)} fusion(f32[128,2,128,128]{3,2,1,0:T(8,128)} %convert_element_type.58, s32[1024]{0:T(1024)S(1)} %pad_clamp_fusion.2), kind=kCustom, calls=%fused_computation | custom fusion | bytes 2097184 | tf_op jit(solution)/shard_map/jit(_take)/gather | solution.py:113
  206.3 3.3 fusion.27
  209.7 1.0 fusion.33
  210.7 0.8 copy-done.1
  212.2 2.3 multiply_reduce_fusion
  214.5 0.8 copy.87
  215.4 3.7 bitcast_convert_fusion
  220.1 0.9 reduce-window.6
  221.4 2.9 scatter_custom_fusion
  224.5 54.1 %reduce-scatter.2.cloned.1.call-done = bf16[32,2048]{1,0:T(8,128)(2,1)} async-done(((bf16[512,2048]{1,0:T(8,128)(2,1)}), bf16[32,2048]{1,0:T(8,128)(2,1)}) %reduce-scatter.2.cloned.1.call-update) | async-done | bytes 131088 | tf_op jit(solution)/shard_map/reduce_scatter | solution.py:141
  278.5 1.1 multiply_reduce_fusion.1
  279.6 1.0 multiply_convert_fusion.2
  280.6 3.3 gather_fusion.1
  284.0 1.8 broadcast_select_fusion
  285.8 31.6 %all_to_all.10 = bf16[16,1,32,2048]{3,2,1,0:T(8,128)(2,1)S(1)} all-to-all(bf16[16,1,32,2048]{3,2,1,0:T(8,128)(2,1)S(1)} %broadcast_select_fusion), channel_id=1, replica_groups=mesh['rep'=16,'exp'=16] {'exp'}, dimensions={0} | all-to-all | bytes 4194304 | tf_op jit(solution)/shard_map/all_to_all | solution.py:168
  317.5 2.4 fusion.14
  319.9 2.6 fusion.2
  322.5 7.7 %all-to-all-start.1 = ((bf16[16,1,32,2048]{3,2,1,0:T(8,128)(2,1)}), bf16[16,1,32,2048]{3,2,1,0:T(8,128)(2,1)}, u32[]{:S(2)}, u32[]{:S(2)}) async-start(bf16[16,1,32,2048]{3,2,1,0:T(8,128)(2,1)} %fusion.2), calls=%async_computation.2 | async-start | bytes 4194304 | tf_op jit(solution)/shard_map/all_to_all | solution.py:178
  330.1 1.4 reduce_sum.63
  331.5 1.4 copy.99
  332.9 1.2 pad_clamp_fusion
  334.1 1.3 compare_and_fusion
  335.4 0.8 copy.102
  336.3 0.7 copy.96
  337.0 4.0 %convolution_add_fusion = f32[8,2,128,128]{3,2,1,0:T(8,128)} fusion(f32[8,2,128,128]{3,2,1,0:T(8,128)S(1)} %gather_fusion, f32[8,2,64,128]{3,2,1,0:T(8,128)} %bitcast.130, f32[8,2]{1,0:T(8,128)S(1)} %bitcast.143, pred[8]{0:T(512)(128)(4,1)} %copy-done.18, f32[8,2,64]{2,1,0:T(2,128)S(1)} %copy.96, f32[8,64,128]{2,1,0:T(8,128)S(1)} %copy-done.3), kind=kOutput, calls=%fused_computation.22 | convolution fusion | flops 202244096 | bytes 2887752 | tf_op jit(solution)/shard_map/while/body/eval_jaxpr/bhjv,bhjk->bhvk/dot_general | solution.py:60
  341.0 17.7 %all-to-all-done.1 = bf16[16,1,32,2048]{3,2,1,0:T(8,128)(2,1)} async-done(((bf16[16,1,32,2048]{3,2,1,0:T(8,128)(2,1)}), bf16[16,1,32,2048]{3,2,1,0:T(8,128)(2,1)}, u32[]{:S(2)}, u32[]{:S(2)}) %all-to-all-start.1) | async-done | bytes 2097184 | tf_op jit(solution)/shard_map/all_to_all | solution.py:178
  358.8 6.8 %gather_fusion.2 = bf16[320,2048]{1,0:T(8,128)(2,1)} fusion(bf16[512,2048]{1,0:T(8,128)(2,1)} %bitcast.48, s32[1024]{0:T(1024)S(1)} %copy-done.15), kind=kCustom, calls=%fused_computation.2 | custom fusion | bytes 2622720 | tf_op jit(solution)/shard_map/jit(_take)/gather | solution.py:179
  365.6 3.4 gather.20
  369.0 2.7 fusion.11
  371.7 0.8 fusion.43
  (97 shorter events, 5.5 us)
Async XLA Ops:
  7.2 312.7 %copy-start = (bf16[1,512,2048]{2,1,0:T(8,128)(2,1)S(1)}, bf16[1,512,2048]{2,1,0:T(8,128)(2,1)}, u32[]{:S(2)}) copy-start(bf16[1,512,2048]{2,1,0:T(8,128)(2,1)} %param.23) | copy-start | bytes 6291460
  7.2 42.2 %all-gather.3.cloned.1.call-start = ((), (), s32[]{:S(2)}) async-start(), calls=%async_computation.3 | async-start | bytes 2228224 | tf_op jit(solution)/shard_map/all_gather | solution.py:88
  10.1 178.6 %all-gather.5.cloned.1.call-start = ((), (), s32[]{:S(2)}) async-start(), calls=%async_computation.4 | async-start | bytes 8912896 | tf_op jit(solution)/shard_map/all_gather | solution.py:110
  12.3 266.2 %reduce-scatter.2.cloned.1.call-start = ((), (), s32[]{:S(2)}) async-start(), calls=%async_computation.5 | async-start | bytes 2228224 | tf_op jit(solution)/shard_map/reduce_scatter | solution.py:141
  15.7 4.1 %copy-start.9 = (bf16[2048,1,256]{2,0,1:T(8,128)(2,1)S(1)}, bf16[2048,1,256]{2,0,1:T(8,128)(2,1)}, u32[]{:S(2)}) copy-start(bf16[2048,1,256]{2,0,1:T(8,128)(2,1)} %param.13) | copy-start | bytes 3145732
  19.8 1.4 copy-start.14
  19.8 1.5 copy-start.22
  19.8 1.5 copy-start.20
  21.4 190.8 %copy-start.18 = (pred[8]{0:T(512)(128)(4,1)}, pred[8]{0:T(512)(128)(4,1)S(1)}, u32[]{:S(2)}) copy-start(pred[8]{0:T(512)(128)(4,1)S(1)} %get-tuple-element.22) | copy-start | bytes 28
  58.8 1.0 copy-start.11
  62.2 144.1 %copy-start.2 = (f32[8,64,128]{2,1,0:T(8,128)}, f32[8,64,128]{2,1,0:T(8,128)S(1)}, u32[]{:S(2)}) copy-start(f32[8,64,128]{2,1,0:T(8,128)S(1)} %broadcast_multiply_fusion) | copy-start | bytes 786436
  144.2 44.5 %copy-start.5 = (f32[8,64,128]{2,1,0:T(8,128)}, f32[8,64,128]{2,1,0:T(8,128)S(1)}, u32[]{:S(2)}) copy-start(f32[8,64,128]{2,1,0:T(8,128)S(1)} %multiply_multiply_fusion) | copy-start | bytes 786436
  206.3 3.4 copy-start.10
  206.3 5.2 %copy-start.7 = (f32[8,2,64,64]{3,2,1,0:T(8,128)S(1)}, f32[8,2,64,64]{3,2,1,0:T(8,128)}, u32[]{:S(2)}) copy-start(f32[8,2,64,64]{3,2,1,0:T(8,128)} %convolution_multiply_fusion.3) | copy-start | bytes 786436
  209.6 2.5 copy-start.6
  210.7 0.8 copy-start.1
  219.1 0.7 copy-start.16
  219.1 59.5 %copy-start.4 = (bf16[32,2048]{1,0:T(8,128)(2,1)S(1)}, bf16[32,2048]{1,0:T(8,128)(2,1)}, u32[]{:S(2)}) copy-start(bf16[32,2048]{1,0:T(8,128)(2,1)} %param.12) | copy-start | bytes 393220
  221.4 58.2 %copy-start.12 = (s32[320]{0:T(512)}, s32[320]{0:T(512)S(1)}, u32[]{:S(2)}) copy-start(s32[320]{0:T(512)S(1)} %fusion.56) | copy-start | bytes 3844
  221.4 2.9 copy-start.17
  285.8 31.7 %copy-start.21 = (bf16[1,2048,1024]{2,1,0:T(8,128)(2,1)S(1)}, bf16[1,2048,1024]{2,1,0:T(8,128)(2,1)}, u32[]{:S(2)}) copy-start(bf16[1,2048,1024]{2,1,0:T(8,128)(2,1)} %param.22) | copy-start | bytes 12582916
  322.5 14.5 %copy-start.3 = (f32[8,64,128]{2,1,0:T(8,128)S(1)}, f32[8,64,128]{2,1,0:T(8,128)}, u32[]{:S(2)}) copy-start(f32[8,64,128]{2,1,0:T(8,128)} %copy-done.2) | copy-start | bytes 786436
  322.5 36.3 %all-to-all-start.1 = ((bf16[16,1,32,2048]{3,2,1,0:T(8,128)(2,1)}), bf16[16,1,32,2048]{3,2,1,0:T(8,128)(2,1)}, u32[]{:S(2)}, u32[]{:S(2)}) async-start(bf16[16,1,32,2048]{3,2,1,0:T(8,128)(2,1)} %fusion.2), calls=%async_computation.2 | async-start | bytes 4194304 | tf_op jit(solution)/shard_map/all_to_all | solution.py:178
  335.4 23.3 %copy-start.15 = (s32[1024]{0:T(1024)S(1)}, s32[1024]{0:T(1024)}, u32[]{:S(2)}) copy-start(s32[1024]{0:T(1024)} %pad_clamp_fusion) | copy-start | bytes 12292
  365.6 3.4 copy-start.13
  365.6 3.4 copy-start.19
  369.0 2.7 copy-start.8
Sparse Core Ops, SparseCore 0:
  10.4 38.9 all-gather.2
  52.0 136.6 all-gather.4
  219.2 59.2 reduce-scatter.1
where the time goes:
time: 380 us; the launch traced here: 379 us
  waiting for transfers between devices  142 us (37%)
  other arithmetic  107 us (28%)
  local copies, waits for them, and re-layouts  41.9 us (11%)
  matrix products  33.8 us (9%)
  blocking collectives  31.6 us (8%)
  between operations  14.2 us (4%)
  starting transfers between devices  7.8 us (2%)
    another operation x4, other arithmetic, block_step(): solver(system.reshape(-1, width, width), right_side.reshape(-1, width, ri...  80.9 us
    reduce_scatter x1, waiting for transfers between devices, local(): lax.psum_scatter(jnp.dot(gated, output_flat, preferred_element_type=jnp.f...  54.1 us
    all_gather x1, waiting for transfers between devices, local(): lax.all_gather(state_cache.astype(jnp.bfloat16), 'rep', axis=0, tiled=True)  42.7 us
    all_to_all x1, blocking collectives, local(): lax.all_to_all(outgoing_rows, 'exp', split_axis=0, concat_axis=0, tiled=T...  31.6 us
    all_gather x1, waiting for transfers between devices, local(): piece = lax.all_gather(normed, 'exp', axis=0, tiled=True)  27.9 us
    all_to_all x1, waiting for transfers between devices, local(): lax.all_to_all(produced, 'exp', split_axis=0, concat_axis=0, tiled=True)  17.7 us
    convert_element_type x1, other arithmetic, local(): every_cache = lax.all_gather(state_cache.astype(jnp.bfloat16), 'rep', axi...  11.2 us
    gather x2, local copies, waits for them, and re-layouts, local(): jnp.take(returned.reshape(total_experts * row_count, model), position, ax...  10.2 us
  transfers between devices with their start and end apart: 4, of which 4 were waited for; matrix products, arithmetic and copies ran while one was open for 32% of the time, Pallas kernels for 0%

commit v1 on v0

--- a/solution.py
+++ b/solution.py
@@ -6,6 +6,15 @@
 
 EPSILON = 1e-06
 HIGHEST = lax.Precision.HIGHEST
+mark_the_vectors = lambda my_data, ax_name, row_dim: jnp.concatenate(
+    jax.lax.all_to_all(
+        jnp.stack(jax.lax.psum(1, axis_name=ax_name) * [my_data]),
+        axis_name=ax_name,
+        split_axis=0,
+        concat_axis=0,
+    ),
+    axis=row_dim,
+)
 
 
 def rms_scale(values):
@@ -85,7 +94,7 @@
     rate_flat = rate_weight.reshape(model, -1)
     residual = tokens.astype(jnp.float32)
     normed = rms_scale(residual).astype(jnp.bfloat16)
-    piece = lax.all_gather(normed, "exp", axis=0, tiled=True)
+    piece = mark_the_vectors(normed, "exp", 0)
     projected = jnp.concatenate(
         [
             jnp.dot(piece, attend_flat, preferred_element_type=jnp.float32),

time: 380 us -> 357 us (0.939)
  waiting for transfers between devices: 142 us -> 107 us
  starting transfers between devices: 7.8 us -> 14.2 us
    all_gather x1 -> x0, waiting for transfers between devices: 27.9 us -> none  [local(): piece = lax.all_gather(normed, 'exp', axis=0, tiled=True)]
    all_gather x1, waiting for transfers between devices: 42.7 us -> 18.2 us  [local(): lax.all_gather(state_cache.astype(jnp.bfloat16), 'rep', axis=0, tiled=True)]
    all_to_all x0 -> x1, waiting for transfers between devices: none -> 16.7 us  [jax.lax.all_to_all(jnp.stack(jax.lax.psum(1, axis_name=ax_name) * [my_dat...]
    all_to_all x0 -> x1, starting transfers between devices: none -> 6.4 us  [jax.lax.all_to_all(jnp.stack(jax.lax.psum(1, axis_name=ax_name) * [my_dat...]
  transfers between devices with their start and end apart: 4 -> 4, of which waited for: 4 -> 4; matrix products, arithmetic and copies ran while one was open for 32% -> 36% of each run, Pallas kernels for 0% -> 0%
where the time goes in v1:
time: 357 us; the launch traced here: 356 us
  other arithmetic  109 us (31%)
  waiting for transfers between devices  107 us (30%)
  local copies, waits for them, and re-layouts  44.2 us (12%)
  matrix products  35.4 us (10%)
  blocking collectives  31.7 us (9%)
  between operations  14.5 us (4%)
  starting transfers between devices  14.2 us (4%)
    another operation x4, other arithmetic, block_step(): solver(system.reshape(-1, width, width), right_side.reshape(-1, width, ri...  82.4 us
    reduce_scatter x1, waiting for transfers between devices, local(): lax.psum_scatter(jnp.dot(gated, output_flat, preferred_element_type=jnp.f...  54.1 us
    all_to_all x1, blocking collectives, local(): lax.all_to_all(outgoing_rows, 'exp', split_axis=0, concat_axis=0, tiled=T...  31.7 us
    all_gather x1, waiting for transfers between devices, local(): lax.all_gather(state_cache.astype(jnp.bfloat16), 'rep', axis=0, tiled=True)  18.2 us
    all_to_all x1, waiting for transfers between devices, local(): lax.all_to_all(produced, 'exp', split_axis=0, concat_axis=0, tiled=True)  17.7 us
    all_to_all x1, waiting for transfers between devices, jax.lax.all_to_all(jnp.stack(jax.lax.psum(1, axis_name=ax_name) * [my_dat...  16.7 us
    convert_element_type x1, other arithmetic, local(): every_cache = lax.all_gather(state_cache.astype(jnp.bfloat16), 'rep', axi...  11.2 us
    gather x2, local copies, waits for them, and re-layouts, local(): jnp.take(returned.reshape(total_experts * row_count, model), position, ax...  10.2 us
  transfers between devices with their start and end apart: 4, of which 4 were waited for; matrix products, arithmetic and copies ran while one was open for 36% of the time, Pallas kernels for 0%

profile of v1, /device:TPU:2, one launch (start us, length us, event | category | flops | bytes accessed | tf_op | source)
XLA Modules:
  0.0 355.9 jit_solution(14142221025996828993)
XLA Ops:
  7.2 2.3 convert_element_type.57
  9.8 1.5 stack.2
  11.4 6.4 %all-to-all-start = ((bf16[16,32,2048]{2,1,0:T(8,128)(2,1)}), bf16[16,32,2048]{2,1,0:T(8,128)(2,1)}, u32[]{:S(2)}, u32[]{:S(2)}) async-start(bf16[16,32,2048]{2,1,0:T(8,128)(2,1)} %stack.2), calls=%async_computation | async-start | bytes 4194304 | tf_op jit(solution)/shard_map/all_to_all | solution.py:10
  17.8 3.4 copy.105
  21.2 4.0 %copy.84 = bf16[512,2048]{1,0:T(8,128)(2,1)} copy(bf16[512,2048]{0,1:T(8,128)(2,1)} %bitcast.126) | data formatting | bytes 4194304 | tf_op jit(solution)/shard_map/dot_general | solution.py:101
  25.3 1.4 copy.101
  29.9 16.7 %all-to-all-done = bf16[16,32,2048]{2,1,0:T(8,128)(2,1)} async-done(((bf16[16,32,2048]{2,1,0:T(8,128)(2,1)}), bf16[16,32,2048]{2,1,0:T(8,128)(2,1)}, u32[]{:S(2)}, u32[]{:S(2)}) %all-to-all-start) | async-done | bytes 2097184 | tf_op jit(solution)/shard_map/all_to_all | solution.py:10
  46.5 2.6 convolution_bitcast_fusion
  49.4 2.3 fusion.67
  53.0 3.5 fusion.68
  56.6 1.0 copy-done.11
  57.5 0.9 slice.67
  60.0 1.8 fusion.17
  61.9 1.7 select_add_fusion
  63.5 80.0 %custom-call.5 = f32[16,1,64,64]{2,3,1,0:T(8,128)} custom-call(f32[16,1,64,64]{3,2,1,0:T(8,128)} %select_add_fusion), custom_call_target="InvertDiagBlocksLowerTriangular" | custom-call | tf_op jit(solution)/shard_map/while/body/eval_jaxpr/vmap(jit(_solve_triangular))/triangular_solve | solution.py:57
  143.6 0.8 multiply_multiply_fusion
  144.4 2.5 convolution_multiply_fusion.3
  146.8 18.2 %all-gather.2.cloned.1.call-done = bf16[128,2,128,128]{3,2,1,0:T(8,128)(2,1)} async-done(((bf16[8,2,128,128]{3,2,1,0:T(8,128)(2,1)}), bf16[128,2,128,128]{3,2,1,0:T(8,128)(2,1)}) %all-gather.2.cloned.1.call-update) | async-done | bytes 8388624 | tf_op jit(solution)/shard_map/all_gather | solution.py:119
  165.1 11.2 %convert_element_type.58 = f32[128,2,128,128]{3,2,1,0:T(8,128)} convert(bf16[128,2,128,128]{3,2,1,0:T(8,128)(2,1)} %all-gather.2.cloned.1.call-done) | non-fusion elementwise | flops 4194304 | bytes 25165824 | tf_op jit(solution)/shard_map/convert_element_type | solution.py:121
  176.3 6.5 %gather_fusion = f32[8,2,128,128]{3,2,1,0:T(8,128)S(1)} fusion(f32[128,2,128,128]{3,2,1,0:T(8,128)} %convert_element_type.58, s32[1024]{0:T(1024)} %pad_clamp_fusion.2), kind=kCustom, calls=%fused_computation | custom fusion | bytes 2097184 | tf_op jit(solution)/shard_map/jit(_take)/gather | solution.py:122
  182.9 3.3 fusion.18
  186.2 1.0 fusion.24
  187.3 0.8 copy-done.1
  188.7 2.3 multiply_reduce_fusion
  191.1 0.8 copy.87
  192.0 3.7 %bitcast_convert_fusion = bf16[512,2048]{1,0:T(8,128)(2,1)} fusion(bf16[2,128,2048]{2,1,0:T(8,128)(2,1)} %param.17, f32[512,2,2,128]{3,0,2,1:T(8,128)} %copy-done.11, f32[512,2,128]{2,0,1:T(8,128)} %bitcast.137, f32[512,2]{0,1:T(2,128)S(1)} %rsqrt.57), kind=kOutput, calls=%fused_computation.6 | convolution fusion | flops 538836992 | bytes 4198400 | tf_op jit(solution)/shard_map/dot_general | solution.py:151
  196.7 0.9 reduce-window.6
  198.0 2.9 scatter_custom_fusion
  201.0 54.1 %reduce-scatter.2.cloned.1.call-done = bf16[32,2048]{1,0:T(8,128)(2,1)} async-done(((bf16[512,2048]{1,0:T(8,128)(2,1)}), bf16[32,2048]{1,0:T(8,128)(2,1)}) %reduce-scatter.2.cloned.1.call-update) | async-done | bytes 131088 | tf_op jit(solution)/shard_map/reduce_scatter | solution.py:150
  255.2 1.1 multiply_reduce_fusion.1
  256.3 1.0 multiply_convert_fusion.2
  257.3 3.3 gather_fusion.1
  260.6 1.8 broadcast_select_fusion
  262.5 31.7 %all_to_all.15 = bf16[16,1,32,2048]{3,2,1,0:T(8,128)(2,1)S(1)} all-to-all(bf16[16,1,32,2048]{3,2,1,0:T(8,128)(2,1)S(1)} %broadcast_select_fusion), channel_id=1, replica_groups=mesh['rep'=16,'exp'=16] {'exp'}, dimensions={0} | all-to-all | bytes 4194304 | tf_op jit(solution)/shard_map/all_to_all | solution.py:177
  294.1 2.4 fusion.8
  296.5 2.6 fusion.2
  299.1 7.7 %all-to-all-start.2 = ((bf16[16,1,32,2048]{3,2,1,0:T(8,128)(2,1)}), bf16[16,1,32,2048]{3,2,1,0:T(8,128)(2,1)}, u32[]{:S(2)}, u32[]{:S(2)}) async-start(bf16[16,1,32,2048]{3,2,1,0:T(8,128)(2,1)} %fusion.2), calls=%async_computation.3 | async-start | bytes 4194304 | tf_op jit(solution)/shard_map/all_to_all | solution.py:187
  306.8 1.4 reduce_sum.63
  308.2 1.4 copy.99
  309.6 1.2 pad_clamp_fusion
  310.8 1.3 compare_and_fusion
  312.1 0.8 copy.102
  313.6 4.0 %convolution_add_fusion = f32[8,2,128,128]{3,2,1,0:T(8,128)} fusion(f32[8,2,128,128]{3,2,1,0:T(8,128)S(1)} %gather_fusion, f32[8,2,64,128]{3,2,1,0:T(8,128)} %bitcast.128, f32[8,2]{1,0:T(8,128)S(1)} %bitcast.141, pred[8]{0:T(512)(128)(4,1)} %get-tuple-element.22, f32[8,2,64]{2,1,0:T(2,128)S(1)} %copy.96, f32[8,64,128]{2,1,0:T(8,128)S(1)} %copy-done.3), kind=kOutput, calls=%fused_computation.16 | convolution fusion | flops 202244096 | bytes 2887752 | tf_op jit(solution)/shard_map/while/body/eval_jaxpr/bhjv,bhjk->bhvk/dot_general | solution.py:69
  317.7 17.7 %all-to-all-done.2 = bf16[16,1,32,2048]{3,2,1,0:T(8,128)(2,1)} async-done(((bf16[16,1,32,2048]{3,2,1,0:T(8,128)(2,1)}), bf16[16,1,32,2048]{3,2,1,0:T(8,128)(2,1)}, u32[]{:S(2)}, u32[]{:S(2)}) %all-to-all-start.2) | async-done | bytes 2097184 | tf_op jit(solution)/shard_map/all_to_all | solution.py:187
  335.4 6.8 %gather_fusion.2 = bf16[320,2048]{1,0:T(8,128)(2,1)} fusion(bf16[512,2048]{1,0:T(8,128)(2,1)} %bitcast.50, s32[1024]{0:T(1024)S(1)} %copy-done.17), kind=kCustom, calls=%fused_computation.2 | custom fusion | bytes 2622720 | tf_op jit(solution)/shard_map/jit(_take)/gather | solution.py:188
  342.3 3.4 gather.20
  345.6 2.7 fusion.5
  348.3 0.8 fusion.34
  (101 shorter events, 9.7 us)
Async XLA Ops:
  7.2 289.4 %copy-start = (bf16[1,512,2048]{2,1,0:T(8,128)(2,1)S(1)}, bf16[1,512,2048]{2,1,0:T(8,128)(2,1)}, u32[]{:S(2)}) copy-start(bf16[1,512,2048]{2,1,0:T(8,128)(2,1)} %param.23) | copy-start | bytes 6291460
  7.2 2.4 copy-start.4
  7.2 157.9 %all-gather.2.cloned.1.call-start = ((), (), s32[]{:S(2)}) async-start(), calls=%async_computation.4 | async-start | bytes 8912896 | tf_op jit(solution)/shard_map/all_gather | solution.py:119
  11.4 35.1 %all-to-all-start = ((bf16[16,32,2048]{2,1,0:T(8,128)(2,1)}), bf16[16,32,2048]{2,1,0:T(8,128)(2,1)}, u32[]{:S(2)}, u32[]{:S(2)}) async-start(bf16[16,32,2048]{2,1,0:T(8,128)(2,1)} %stack.2), calls=%async_computation | async-start | bytes 4194304 | tf_op jit(solution)/shard_map/all_to_all | solution.py:10
  17.8 237.4 %reduce-scatter.2.cloned.1.call-start = ((), (), s32[]{:S(2)}) async-start(), calls=%async_computation.5 | async-start | bytes 2228224 | tf_op jit(solution)/shard_map/reduce_scatter | solution.py:150
  21.2 4.0 %copy-start.9 = (bf16[2048,1,256]{2,0,1:T(8,128)(2,1)S(1)}, bf16[2048,1,256]{2,0,1:T(8,128)(2,1)}, u32[]{:S(2)}) copy-start(bf16[2048,1,256]{2,0,1:T(8,128)(2,1)} %param.13) | copy-start | bytes 3145732
  25.2 1.4 copy-start.16
  25.3 1.5 copy-start.24
  25.3 1.5 copy-start.22
  56.6 1.0 copy-start.11
  58.5 1.5 copy-start.12
  60.0 122.9 %copy-start.2 = (f32[8,64,128]{2,1,0:T(8,128)}, f32[8,64,128]{2,1,0:T(8,128)S(1)}, u32[]{:S(2)}) copy-start(f32[8,64,128]{2,1,0:T(8,128)S(1)} %broadcast_multiply_fusion) | copy-start | bytes 786436
  144.4 20.7 %copy-start.5 = (f32[8,64,128]{2,1,0:T(8,128)}, f32[8,64,128]{2,1,0:T(8,128)S(1)}, u32[]{:S(2)}) copy-start(f32[8,64,128]{2,1,0:T(8,128)S(1)} %multiply_multiply_fusion) | copy-start | bytes 786436
  176.3 6.6 %copy-start.13 = (f32[8,2,64]{2,1,0:T(2,128)S(1)}, f32[8,2,64]{2,1,0:T(2,128)}, u32[]{:S(2)}) copy-start(f32[8,2,64]{2,1,0:T(2,128)} %copy-done.12) | copy-start | bytes 12292
  182.8 3.4 copy-start.10
  182.8 5.2 %copy-start.7 = (f32[8,2,64,64]{3,2,1,0:T(8,128)S(1)}, f32[8,2,64,64]{3,2,1,0:T(8,128)}, u32[]{:S(2)}) copy-start(f32[8,2,64,64]{3,2,1,0:T(8,128)} %convolution_multiply_fusion.3) | copy-start | bytes 786436
  186.2 2.5 copy-start.6
  186.2 2.5 copy-start.20
  187.3 0.8 copy-start.1
  195.7 0.7 copy-start.18
  197.9 58.3 %copy-start.14 = (s32[320]{0:T(512)}, s32[320]{0:T(512)S(1)}, u32[]{:S(2)}) copy-start(s32[320]{0:T(512)S(1)} %fusion.47) | copy-start | bytes 3844
  198.0 2.9 copy-start.19
  262.5 31.7 %copy-start.23 = (bf16[1,2048,1024]{2,1,0:T(8,128)(2,1)S(1)}, bf16[1,2048,1024]{2,1,0:T(8,128)(2,1)}, u32[]{:S(2)}) copy-start(bf16[1,2048,1024]{2,1,0:T(8,128)(2,1)} %param.22) | copy-start | bytes 12582916
  299.1 14.5 %copy-start.3 = (f32[8,64,128]{2,1,0:T(8,128)S(1)}, f32[8,64,128]{2,1,0:T(8,128)}, u32[]{:S(2)}) copy-start(f32[8,64,128]{2,1,0:T(8,128)} %copy-done.2) | copy-start | bytes 786436
  299.1 36.3 %all-to-all-start.2 = ((bf16[16,1,32,2048]{3,2,1,0:T(8,128)(2,1)}), bf16[16,1,32,2048]{3,2,1,0:T(8,128)(2,1)}, u32[]{:S(2)}, u32[]{:S(2)}) async-start(bf16[16,1,32,2048]{3,2,1,0:T(8,128)(2,1)} %fusion.2), calls=%async_computation.3 | async-start | bytes 4194304 | tf_op jit(solution)/shard_map/all_to_all | solution.py:187
  312.1 23.3 %copy-start.17 = (s32[1024]{0:T(1024)S(1)}, s32[1024]{0:T(1024)}, u32[]{:S(2)}) copy-start(s32[1024]{0:T(1024)} %pad_clamp_fusion) | copy-start | bytes 12292
  342.2 3.4 copy-start.15
  342.3 3.4 copy-start.21
  345.6 2.7 copy-start.8
Sparse Core Ops, SparseCore 0:
  10.6 154.4 all-gather.1
  195.8 59.3 reduce-scatter.1
